TPU v7x, 128 devices: a whole 4x4x4 slice. The times are simulated.
128 devices in a mesh: rows: 16 (over y, z), seq: 8 (over x, core).
Axes of the slice: x: 4, y: 4, z: 4, core: 2. Of those that a mesh axis runs over, the one named last changes fastest.
Arguments:
- residual_in: bfloat16 [16, 2048, 3200], P('rows', 'seq'), may hold values from -6 to 6
- norm_gain: float32 [3200], replicated, may hold values from 0.1 to 1.9
- qkv_weight: bfloat16 [3200, 6144], P(None, 'seq')
- qk_gain: float32 [2, 2048], P(None, 'seq')
- out_weight: bfloat16 [2048, 3200], P('seq'), may hold values from -0.125 to 0.125
- layer_scale: float32 [3200], replicated, may hold values from 1 to 6
- segment_ids: int32 [16, 2048], P('rows', 'seq'), may hold values from 0 to 2, as said below
- pad_mask: int32 [16, 2048], P('rows', 'seq'), may hold values from 0 to 1, as said below
- ln_weight: float32 [12800], replicated, may hold values from 0.1 to 1.9
- ln_bias: float32 [12800], replicated, may hold values from -3 to 3
- fc_weight: bfloat16 [12800, 6144], P('rows'), may hold values from -0.0546875 to 0.0546875
- fc_bias: float32 [6144], replicated, may hold values from -3 to 3
- owner: int32 [16], replicated, may hold values from 0 to 15, each once
Outputs:
- features: bfloat16 [16, 512, 6144], P('rows', 'seq')
Inputs may be any that keep to these rules, and one draw needn't show every extreme that they name: `segment_ids`: within a row, segment ids never fall and change only at multiples of 1024 tokens; picture tokens carry ids below 2, padding tokens carry 2 and stand at the end of the row; the first tile is never padding. pad_mask is 0 exactly where segment_ids equals 2. `owner`: each index of rows owns exactly one row.
All inputs are finite; a program needn't handle non-finite values.
Results may differ from a plain program's by a relative error of at most 0.025.
Values may be sent and summed in bfloat16 or wider, within the bound.
A program may use at most 128 MiB of HBM per device.

v0:
```python
import jax
import jax.numpy as jnp
from jax import lax
from jax.sharding import PartitionSpec as P

D = 3200
HEAD_DIM = 128
HEADS = 16
GRID = 32
MASK_SHIFT = 1000000.0


def attend_dense(query_norm, key_norm, value_half, row_segments, block_len, scale):
    length, heads_here = (query_norm.shape[0], query_norm.shape[1])
    block_count = length // block_len

    def one_block(packed):
        query_block, query_seg = packed
        scores = (
            jnp.einsum("qhd,khd->hqk", query_block, key_norm, preferred_element_type=jnp.float32)
            * scale
        )
        same_seg = (query_seg[:, None] == row_segments[None, :])[None]
        scores = jnp.where(same_seg, scores, -1e30)
        peak_val = jnp.max(scores, axis=-1, keepdims=True)
        exp_terms = jnp.exp(scores - peak_val)
        probs = (exp_terms / jnp.sum(exp_terms, axis=-1, keepdims=True)).astype(jnp.bfloat16)
        return jnp.einsum(
            "hqk,khd->qhd", probs, value_half, preferred_element_type=jnp.float32
        ).astype(jnp.bfloat16)

    blocks_out = lax.map(
        one_block,
        (
            query_norm.reshape(block_count, block_len, heads_here, HEAD_DIM),
            row_segments.reshape(block_count, block_len),
        ),
    )
    return blocks_out.reshape(length, heads_here * HEAD_DIM)


def per_device(
    residual_in,
    norm_gain,
    qkv_weight,
    qk_gain,
    out_weight,
    layer_scale,
    segment_ids,
    pad_mask,
    ln_weight,
    ln_bias,
    fc_weight,
    fc_bias,
    owner,
):
    seq_count = lax.axis_size("seq")
    seq_me = lax.axis_index("seq")
    tokens = residual_in[0].astype(jnp.float32)
    shard_rows = tokens.shape[0]
    normed = (
        tokens * lax.rsqrt(jnp.mean(tokens * tokens, axis=-1, keepdims=True) + 1e-06) * norm_gain
    ).astype(jnp.bfloat16)
    row_tokens = lax.all_gather(normed, "seq", axis=0, tiled=True)
    length = row_tokens.shape[0]
    heads_here = qkv_weight.shape[1] // (3 * HEAD_DIM)
    projected = jnp.dot(row_tokens, qkv_weight, preferred_element_type=jnp.float32).reshape(
        length, heads_here, 3, HEAD_DIM
    )
    query_raw = projected[:, :, 0]
    key_raw = projected[:, :, 1]
    value_half = projected[:, :, 2].astype(jnp.bfloat16)
    seg_spread = lax.dynamic_update_slice_in_dim(
        jnp.zeros((length,), jnp.float32),
        segment_ids[0].astype(jnp.float32),
        seq_me * shard_rows,
        0,
    )
    stats = lax.psum(
        jnp.stack(
            [
                jnp.sum(query_raw * query_raw, axis=(1, 2)),
                jnp.sum(key_raw * key_raw, axis=(1, 2)),
                seg_spread,
            ]
        ),
        "seq",
    )
    query_sq, key_sq, row_segments = (stats[0], stats[1], stats[2])
    norm_width = HEADS * HEAD_DIM
    gain_pair = qk_gain.reshape(2, heads_here, HEAD_DIM)
    query_norm = (
        query_raw * lax.rsqrt(query_sq / norm_width + 1e-06)[:, None, None] * gain_pair[0]
    ).astype(jnp.bfloat16)
    key_norm = (
        key_raw * lax.rsqrt(key_sq / norm_width + 1e-06)[:, None, None] * gain_pair[1]
    ).astype(jnp.bfloat16)
    block_len = min(512, length)
    scale = HEAD_DIM ** (-0.5)
    attended = attend_dense(query_norm, key_norm, value_half, row_segments, block_len, scale)
    group_width = attended.shape[1]
    own_heads = lax.all_to_all(attended.reshape(seq_count, shard_rows, group_width), "seq", 0, 0)
    full_out_weight = lax.all_gather(out_weight, "seq", axis=0, tiled=False)
    group_terms = jnp.einsum(
        "gtc,gcd->gtd", own_heads, full_out_weight, preferred_element_type=jnp.float32
    ).astype(jnp.bfloat16)
    attn = jnp.sum(group_terms.astype(jnp.float32), axis=0)
    hidden = tokens + layer_scale * attn
    half_grid = GRID // 2
    lines = shard_rows // (2 * GRID)
    merged_count = shard_rows // 4
    merged = jnp.transpose(hidden.reshape(lines, 2, half_grid, 2, D), (0, 2, 1, 3, 4)).reshape(
        merged_count, 4 * D
    )
    centre = merged - jnp.mean(merged, axis=-1, keepdims=True)
    spread = jnp.mean(centre * centre, axis=-1, keepdims=True)
    merged_norm = (centre * lax.rsqrt(spread + 1e-05) * ln_weight + ln_bias).astype(jnp.bfloat16)
    merged_mask = (
        pad_mask[0]
        .reshape(lines, 2, half_grid, 2)[:, 0, :, 0]
        .reshape(merged_count)
        .astype(jnp.float32)
    )
    row_count = lax.axis_size("rows")
    row_me = lax.axis_index("rows")
    slabs = lax.all_to_all(merged_norm, "rows", split_axis=1, concat_axis=0, tiled=True)
    owner_hot = (owner[None, :] == jnp.arange(row_count, dtype=jnp.int32)[:, None]).astype(
        jnp.bfloat16
    )
    ordered = jnp.einsum(
        "jp,pms->jms",
        owner_hot,
        slabs.reshape(row_count, merged_count, -1),
        preferred_element_type=jnp.float32,
    ).astype(jnp.bfloat16)
    ordered = ordered.reshape(row_count * merged_count, -1)
    partial = jnp.dot(ordered, fc_weight, preferred_element_type=jnp.float32).reshape(
        row_count, merged_count, -1
    )
    own_slot = (jnp.arange(row_count, dtype=jnp.int32) == owner[row_me]).astype(jnp.float32)
    shift = own_slot[:, None] * ((merged_mask - 1.0) * MASK_SHIFT)[None, :]
    partial = (partial + shift[:, :, None]).astype(jnp.bfloat16)
    summed = lax.psum_scatter(
        partial.reshape(row_count * merged_count, -1), "rows", scatter_dimension=0, tiled=True
    ).astype(jnp.float32)
    result = jax.nn.gelu(summed + fc_bias, approximate=False)
    return result.astype(jnp.bfloat16)[None]


def solution(mesh):
    return jax.shard_map(
        per_device,
        mesh=mesh,
        in_specs=(
            P("rows", "seq", None),
            P(),
            P(None, "seq"),
            P(None, "seq"),
            P("seq", None),
            P(),
            P("rows", "seq"),
            P("rows", "seq"),
            P(),
            P(),
            P("rows", None),
            P(),
            P(),
        ),
        out_specs=P("rows", "seq", None),
        check_vma=False,
    )
```

profile of v0, /device:TPU:1, one launch (start us, length us, event | category | flops | bytes accessed | tf_op | source)
XLA Modules:
  0.0 404.6 jit_solution(10836090393352335551)
XLA Ops:
  6.5 2.0 fusion.28
  8.5 2.4 fusion.30
  11.0 0.7 all-gather.6.cloned.1.call-update
  11.7 72.5 %all-gather.4.cloned.1.call-done = bf16[2048,3200]{1,0:T(8,128)(2,1)} async-done(((bf16[256,3200]{1,0:T(8,128)(2,1)}), bf16[2048,3200]{1,0:T(8,128)(2,1)}) %all-gather.4.cloned.1.call-update) | async-done | bytes 13107216 | tf_op jit(solution)/shard_map/all_gather | solution.py:64
  84.2 15.7 %fusion.74 = f32[2048,768]{0,1:T(8,128)S(1)} fusion(bf16[2048,3200]{1,0:T(8,128)(2,1)} %all-gather.4.cloned.1.call-done, bf16[3200,768]{1,0:T(8,128)(2,1)} %param.17), kind=kOutput, calls=%fused_computation.97 | convolution fusion | flops 10066329600 | bytes 24313856 | tf_op jit(solution)/shard_map/dot_general | solution.py:67
  99.9 0.1 slice.44
  100.1 2.5 fusion.72
  102.5 1.9 copy.44
  104.4 2.9 copy.43
  107.3 0.3 fusion.31
  107.7 1.3 copy-done
  108.9 0.3 multiply_reduce_fusion.1
  109.3 22.6 %psum.7 = f32[3,2048]{1,0:T(4,128)S(1)} all-reduce(f32[3,2048]{1,0:T(4,128)S(1)} %pad_maximum_fusion), channel_id=1, replica_groups=mesh['rows'=16,'seq'=8] {'seq'}, use_global_device_ids=true, to_apply=%region_3.0 | all-reduce | flops 6144 | bytes 49152 | tf_op jit(solution)/shard_map/psum | solution.py:79
  131.9 0.1 fusion.62
  132.0 1.3 copy.45
  133.3 3.0 multiply_convert_fusion
  136.3 1.3 fusion.33
  137.6 53.7 %while.10 = (s32[]{:T(128)}, bf16[4,512,2,128]{3,2,1,0:T(2,128)(2,1)S(1)}, f32[4,512]{1,0:T(4,128)S(1)}, f32[1,2048]{1,0:T(1,128)S(1)}, bf16[4,512,2,128]{3,1,0,...) while((s32[]{:T(128)}, ...), condition=%wide.region_7.8_spmd, body=%wide.region_4.7_spmd.sunk | while | flops 1087506432 | bytes 26237560 | solution.py:32
  137.6 0.7 broadcast_compare_fusion.2
  138.3 7.8 %fusion.90 = (f32[2,512]{1,0:T(2,128)S(1)}, f32[2,512,2048]{2,1,0:T(8,128)}) fusion(pred[512,2048]{1,0:T(8,128)(4,1)S(1)} %broadcast_compare_fusion.2, bf16[2048,2,128]{2,0,1:T(8,128)(2,1)} %get-tuple-element.158, bf16[4,512,2,128]{3,1,0,2:T(8,128)(2,1)} %get-tuple-element.157, s32[]{:T(128)} %get-tuple-element.145), kind=kOutput, calls=%fused_computation.94.clone.1 | convolution fusion | flops 545261568 | bytes 10752512 | tf_op jit(solution)/shard_map/while/body/eval_jaxpr/sub | solution.py:26
  146.1 4.7 %fusion.91 = bf16[1,512,2,128]{3,1,2,0:T(8,128)(2,1)S(1)} fusion(bf16[2048,2,128]{2,0,1:T(8,128)(2,1)S(1)} %copy-done.5, f32[2,512,2048]{2,1,0:T(8,128)} %get-tuple-element.135, f32[2,512]{1,0:T(2,128)S(1)} %get-tuple-element.136), kind=kOutput, calls=%fused_computation.11.clone.1 | convolution fusion | flops 541196288 | bytes 9703424 | tf_op jit(solution)/shard_map/while/body/eval_jaxpr/hqk,khd->qhd/dot_general | solution.py:28
  150.8 0.3 copy_dynamic-update-slice_fusion.2
  151.1 0.7 broadcast_compare_fusion.2
  151.8 7.7 %fusion.90 = (f32[2,512]{1,0:T(2,128)S(1)}, f32[2,512,2048]{2,1,0:T(8,128)}) fusion(pred[512,2048]{1,0:T(8,128)(4,1)S(1)} %broadcast_compare_fusion.2, bf16[2048,2,128]{2,0,1:T(8,128)(2,1)} %get-tuple-element.158, bf16[4,512,2,128]{3,1,0,2:T(8,128)(2,1)} %get-tuple-element.157, s32[]{:T(128)} %get-tuple-element.145), kind=kOutput, calls=%fused_computation.94.clone.1 | convolution fusion | flops 545261568 | bytes 10752512 | tf_op jit(solution)/shard_map/while/body/eval_jaxpr/sub | solution.py:26
  159.5 4.7 %fusion.91 = bf16[1,512,2,128]{3,1,2,0:T(8,128)(2,1)S(1)} fusion(bf16[2048,2,128]{2,0,1:T(8,128)(2,1)S(1)} %copy-done.5, f32[2,512,2048]{2,1,0:T(8,128)} %get-tuple-element.135, f32[2,512]{1,0:T(2,128)S(1)} %get-tuple-element.136), kind=kOutput, calls=%fused_computation.11.clone.1 | convolution fusion | flops 541196288 | bytes 9703424 | tf_op jit(solution)/shard_map/while/body/eval_jaxpr/hqk,khd->qhd/dot_general | solution.py:28
  164.2 0.3 copy_dynamic-update-slice_fusion.2
  164.5 0.7 broadcast_compare_fusion.2
  165.2 7.7 %fusion.90 = (f32[2,512]{1,0:T(2,128)S(1)}, f32[2,512,2048]{2,1,0:T(8,128)}) fusion(pred[512,2048]{1,0:T(8,128)(4,1)S(1)} %broadcast_compare_fusion.2, bf16[2048,2,128]{2,0,1:T(8,128)(2,1)} %get-tuple-element.158, bf16[4,512,2,128]{3,1,0,2:T(8,128)(2,1)} %get-tuple-element.157, s32[]{:T(128)} %get-tuple-element.145), kind=kOutput, calls=%fused_computation.94.clone.1 | convolution fusion | flops 545261568 | bytes 10752512 | tf_op jit(solution)/shard_map/while/body/eval_jaxpr/sub | solution.py:26
  172.9 4.7 %fusion.91 = bf16[1,512,2,128]{3,1,2,0:T(8,128)(2,1)S(1)} fusion(bf16[2048,2,128]{2,0,1:T(8,128)(2,1)S(1)} %copy-done.5, f32[2,512,2048]{2,1,0:T(8,128)} %get-tuple-element.135, f32[2,512]{1,0:T(2,128)S(1)} %get-tuple-element.136), kind=kOutput, calls=%fused_computation.11.clone.1 | convolution fusion | flops 541196288 | bytes 9703424 | tf_op jit(solution)/shard_map/while/body/eval_jaxpr/hqk,khd->qhd/dot_general | solution.py:28
  177.6 0.3 copy_dynamic-update-slice_fusion.2
  177.9 0.7 broadcast_compare_fusion.2
  178.6 7.7 %fusion.90 = (f32[2,512]{1,0:T(2,128)S(1)}, f32[2,512,2048]{2,1,0:T(8,128)}) fusion(pred[512,2048]{1,0:T(8,128)(4,1)S(1)} %broadcast_compare_fusion.2, bf16[2048,2,128]{2,0,1:T(8,128)(2,1)} %get-tuple-element.158, bf16[4,512,2,128]{3,1,0,2:T(8,128)(2,1)} %get-tuple-element.157, s32[]{:T(128)} %get-tuple-element.145), kind=kOutput, calls=%fused_computation.94.clone.1 | convolution fusion | flops 545261568 | bytes 10752512 | tf_op jit(solution)/shard_map/while/body/eval_jaxpr/sub | solution.py:26
  186.3 4.7 %fusion.91 = bf16[1,512,2,128]{3,1,2,0:T(8,128)(2,1)S(1)} fusion(bf16[2048,2,128]{2,0,1:T(8,128)(2,1)S(1)} %copy-done.5, f32[2,512,2048]{2,1,0:T(8,128)} %get-tuple-element.135, f32[2,512]{1,0:T(2,128)S(1)} %get-tuple-element.136), kind=kOutput, calls=%fused_computation.11.clone.1 | convolution fusion | flops 541196288 | bytes 9703424 | tf_op jit(solution)/shard_map/while/body/eval_jaxpr/hqk,khd->qhd/dot_general | solution.py:28
  191.0 0.3 copy_dynamic-update-slice_fusion.2
  191.3 1.5 reshape_reshape.3
  192.8 7.8 %all-to-all-start = ((bf16[8,256,256]{2,1,0:T(8,128)(2,1)}), bf16[8,256,256]{2,1,0:T(8,128)(2,1)S(1)}, u32[]{:S(2)}, u32[]{:S(2)}) async-start(bf16[8,256,256]{2,1,0:T(8,128)(2,1)} %reshape_reshape.3), calls=%async_computation | async-start | bytes 2097152 | tf_op jit(solution)/shard_map/all_to_all | solution.py:102
  200.6 2.8 reshape.214
  203.4 0.1 add.97
  203.5 0.1 mul.171
  203.7 12.1 %all-to-all-done = bf16[8,256,256]{2,1,0:T(8,128)(2,1)S(1)} async-done(((bf16[8,256,256]{2,1,0:T(8,128)(2,1)}), bf16[8,256,256]{2,1,0:T(8,128)(2,1)S(1)}, u32[]{:S(2)}, u32[]{:S(2)}) %all-to-all-start) | async-done | bytes 1048608 | tf_op jit(solution)/shard_map/all_to_all | solution.py:102
  215.7 10.6 %convert_reduce_fusion = f32[256,3200]{1,0:T(8,128)} fusion(bf16[8,256,256]{2,1,0:T(8,128)(2,1)S(1)} %all-to-all-done, bf16[8,256,3200]{2,1,0:T(8,128)(2,1)} %bitcast.99), kind=kOutput, calls=%fused_computation.24 | convolution fusion | flops 3374284800 | bytes 17432576 | tf_op jit(solution)/shard_map/gtc,gcd->gtd/dot_general | solution.py:104
  226.3 5.3 %reduce_sum.69 = f32[4,2,16,2,3200]{4,3,2,1,0:T(2,128)} reshape(f32[256,3200]{1,0:T(8,128)} %convert_reduce_fusion) | data formatting | bytes 6553600 | tf_op jit(solution)/shard_map/reduce_sum | solution.py:107
  231.7 4.2 %fusion.66 = (f32[4,16]{1,0:T(4,128)S(1)}, f32[4,16,2,2,3200]{4,3,1,2,0:T(2,128)S(1)}) fusion(f32[4,2,16,2,3200]{4,3,2,1,0:T(2,128)S(1)} %copy-done.3, f32[4,2,16,2,3200]{4,3,2,1,0:T(2,128)} %reduce_sum.69, f32[3200]{0:T(1024)S(1)} %copy-done.9), kind=kLoop, calls=%fused_computation.93 | loop fusion | flops 2457536 | bytes 9843456 | tf_op jit(solution)/shard_map/reduce_sum | solution.py:115
  235.9 0.3 copy.36
  236.2 1.9 multiply_reduce_fusion
  238.1 0.1 div.33
  238.2 0.1 rsqrt.45
  238.3 4.5 %reshape.212 = f32[64,16,800]{2,1,0:T(8,128)} reshape(f32[4,16,2,2,3200]{4,3,2,1,0:T(2,128)S(1)} %copy.36) | data formatting | bytes 6553600 | tf_op jit(solution)/shard_map/reshape | solution.py:112
  242.7 2.7 add_convert_fusion.1
  245.5 1.7 copy.37
  247.1 7.0 %all-to-all-start.1 = ((bf16[64,16,800]{2,0,1:T(8,128)(2,1)}), bf16[64,16,800]{2,0,1:T(8,128)(2,1)S(1)}, u32[]{:S(2)}, u32[]{:S(2)}) async-start(bf16[64,16,800]{2,0,1:T(8,128)(2,1)} %copy.37), calls=%async_computation.1 | async-start | bytes 3670016 | tf_op jit(solution)/shard_map/all_to_all | solution.py:126
  254.2 0.5 broadcast.188
  254.7 0.7 reduce.16
  255.4 0.1 reshape_squeeze.8
  255.5 0.1 fusion.57
  255.6 0.1 mul.177
  255.7 0.6 dynamic_slice.11
  256.3 0.6 compare_convert_fusion
  257.0 0.1 broadcast_multiply_fusion
  257.0 20.2 %all-to-all-done.1 = bf16[64,16,800]{2,0,1:T(8,128)(2,1)S(1)} async-done(((bf16[64,16,800]{2,0,1:T(8,128)(2,1)}), bf16[64,16,800]{2,0,1:T(8,128)(2,1)S(1)}, u32[]{:S(2)}, u32[]{:S(2)}) %all-to-all-start.1) | async-done | bytes 1638432 | tf_op jit(solution)/shard_map/all_to_all | solution.py:126
  277.2 1.3 fusion.38
  278.5 19.2 %add_convert_fusion = bf16[16,64,6144]{2,1,0:T(8,128)(2,1)} fusion(f32[16,64]{1,0:T(8,128)S(1)} %broadcast_multiply_fusion, bf16[800,6144]{1,0:T(8,128)(2,1)} %param.25, bf16[16,64,800]{2,0,1:T(8,128)(2,1)S(1)} %fusion.38), kind=kOutput, calls=%fused_computation.25 | convolution fusion | flops 10078912512 | bytes 24055808 | tf_op jit(solution)/shard_map/dot_general | solution.py:137
  297.8 95.1 %reduce-scatter.2.cloned.1.call-done = bf16[64,6144]{1,0:T(8,128)(2,1)} async-done(((bf16[1024,6144]{1,0:T(8,128)(2,1)}), bf16[64,6144]{1,0:T(8,128)(2,1)}) %reduce-scatter.2.cloned.1.call-update) | async-done | bytes 786448 | tf_op jit(solution)/shard_map/reduce_scatter | solution.py:143
  392.9 5.2 %fusion.54 = bf16[1,64,6144]{2,1,0:T(8,128)(2,1)} fusion(bf16[64,6144]{1,0:T(8,128)(2,1)} %reduce-scatter.2.cloned.1.call-done, f32[6144]{0:T(1024)S(1)} %copy-done.8), kind=kLoop, calls=%fused_computation.70 | loop fusion | flops 26345472 | bytes 1597440 | tf_op jit(solution)/shard_map/broadcast_in_dim | solution.py:147
  (53 shorter events, 0.3 us)
Async XLA Ops:
  6.5 2.0 copy-start.1
  6.5 77.7 %all-gather.4.cloned.1.call-start = ((), (), s32[]{:S(2)}) async-start(), calls=%async_computation.3 | async-start | bytes 14745600 | tf_op jit(solution)/shard_map/all_gather | solution.py:64
  10.9 0.8 copy-start.11
  10.9 0.8 copy-start.10
  10.9 192.8 %all-gather.6.cloned.1.call-start = ((), (), s32[]{:S(2)}) async-start(), calls=%async_computation.5 | async-start | bytes 14745600 | tf_op jit(solution)/shard_map/all_gather | solution.py:103
  107.3 1.6 copy-start
  136.3 1.3 copy-start.4
  138.3 7.8 %copy-start.5 = (bf16[2048,2,128]{2,0,1:T(8,128)(2,1)S(1)}, bf16[2048,2,128]{2,0,1:T(8,128)(2,1)}, u32[]{:S(2)}) copy-start(bf16[2048,2,128]{2,0,1:T(8,128)(2,1)} %get-tuple-element.159) | copy-start | bytes 3145732 | tf_op jit(solution)/shard_map/while
  151.7 7.8 %copy-start.5 = (bf16[2048,2,128]{2,0,1:T(8,128)(2,1)S(1)}, bf16[2048,2,128]{2,0,1:T(8,128)(2,1)}, u32[]{:S(2)}) copy-start(bf16[2048,2,128]{2,0,1:T(8,128)(2,1)} %get-tuple-element.159) | copy-start | bytes 3145732 | tf_op jit(solution)/shard_map/while
  165.2 7.8 %copy-start.5 = (bf16[2048,2,128]{2,0,1:T(8,128)(2,1)S(1)}, bf16[2048,2,128]{2,0,1:T(8,128)(2,1)}, u32[]{:S(2)}) copy-start(bf16[2048,2,128]{2,0,1:T(8,128)(2,1)} %get-tuple-element.159) | copy-start | bytes 3145732 | tf_op jit(solution)/shard_map/while
  178.6 7.8 %copy-start.5 = (bf16[2048,2,128]{2,0,1:T(8,128)(2,1)S(1)}, bf16[2048,2,128]{2,0,1:T(8,128)(2,1)}, u32[]{:S(2)}) copy-start(bf16[2048,2,128]{2,0,1:T(8,128)(2,1)} %get-tuple-element.159) | copy-start | bytes 3145732 | tf_op jit(solution)/shard_map/while
  191.3 9.3 %copy-start.2 = (bf16[1,256,3200]{2,1,0:T(8,128)(2,1)S(1)}, bf16[1,256,3200]{2,1,0:T(8,128)(2,1)}, u32[]{:S(2)}) copy-start(bf16[1,256,3200]{2,1,0:T(8,128)(2,1)} %param.15) | copy-start | bytes 4915204
  192.8 22.9 %all-to-all-start = ((bf16[8,256,256]{2,1,0:T(8,128)(2,1)}), bf16[8,256,256]{2,1,0:T(8,128)(2,1)S(1)}, u32[]{:S(2)}, u32[]{:S(2)}) async-start(bf16[8,256,256]{2,1,0:T(8,128)(2,1)} %reshape_reshape.3), calls=%async_computation | async-start | bytes 2097152 | tf_op jit(solution)/shard_map/all_to_all | solution.py:102
  200.6 2.8 copy-start.6
  200.6 2.9 copy-start.7
  226.3 5.3 %copy-start.3 = (f32[4,2,16,2,3200]{4,3,2,1,0:T(2,128)S(1)}, f32[4,2,16,2,3200]{4,3,2,1,0:T(2,128)}, u32[]{:S(2)}) copy-start(f32[4,2,16,2,3200]{4,3,2,1,0:T(2,128)} %reshape.214) | copy-start | bytes 9830404
  226.3 5.3 %copy-start.9 = (f32[3200]{0:T(1024)S(1)}, f32[3200]{0:T(1024)}, u32[]{:S(2)}) copy-start(f32[3200]{0:T(1024)} %param.20) | copy-start | bytes 38404
  247.1 7.6 %copy-start.12 = (s32[1,256]{1,0:T(1,128)S(1)}, s32[1,256]{1,0:T(1,128)}, u32[]{:S(2)}) copy-start(s32[1,256]{1,0:T(1,128)} %param.22) | copy-start | bytes 3076
  247.1 8.6 %copy-start.13 = (s32[16]{0:T(128)S(1)}, s32[16]{0:T(128)}, u32[]{:S(2)}) copy-start(s32[16]{0:T(128)} %param.27) | copy-start | bytes 196
  247.1 30.1 %all-to-all-start.1 = ((bf16[64,16,800]{2,0,1:T(8,128)(2,1)}), bf16[64,16,800]{2,0,1:T(8,128)(2,1)S(1)}, u32[]{:S(2)}, u32[]{:S(2)}) async-start(bf16[64,16,800]{2,0,1:T(8,128)(2,1)} %copy.37), calls=%async_computation.1 | async-start | bytes 3670016 | tf_op jit(solution)/shard_map/all_to_all | solution.py:126
  254.2 138.7 %reduce-scatter.2.cloned.1.call-start = ((), (), s32[]{:S(2)}) async-start(), calls=%async_computation.4 | async-start | bytes 13369344 | tf_op jit(solution)/shard_map/reduce_scatter | solution.py:143
  297.7 95.1 %copy-start.8 = (f32[6144]{0:T(1024)S(1)}, f32[6144]{0:T(1024)}, u32[]{:S(2)}) copy-start(f32[6144]{0:T(1024)} %param.26) | copy-start | bytes 73732
Sparse Core Ops, SparseCore 0:
  11.0 73.1 all-gather.3
  85.9 70.2 all-gather.5
  297.9 94.9 reduce-scatter.1
where the time goes:
time: 405 us
  waiting for transfers between devices  201 us (50%)
  matrix products  96.5 us (24%)
  local copies, waits for them, and re-layouts  29 us (7%)
  other arithmetic  27.6 us (7%)
  blocking collectives  22.6 us (6%)
  starting transfers between devices  14.9 us (4%)
  between operations  13.3 us (3%)
    reduce_scatter x1, waiting for transfers between devices, per_device(): lax.psum_scatter(partial.reshape(row_count * merged_count, -1), 'rows', s...  95.1 us
    all_gather x1, waiting for transfers between devices, per_device(): row_tokens = lax.all_gather(normed, 'seq', axis=0, tiled=True)  72.5 us
    sub x4, matrix products, one_block(): exp_terms = jnp.exp(scores - peak_val)  31 us
    psum x1, blocking collectives, per_device(): lax.psum(jnp.stack([jnp.sum(query_raw * query_raw, axis=(1, 2)), jnp.sum(...  22.6 us
    all_to_all x1, waiting for transfers between devices, per_device(): lax.all_to_all(merged_norm, 'rows', split_axis=1, concat_axis=0, tiled=True)  20.2 us
    dot_general x1, matrix products, per_device(): jnp.dot(ordered, fc_weight, preferred_element_type=jnp.float32)  19.2 us
    dot_general x4, matrix products, one_block(): jnp.einsum('hqk,khd->qhd', probs, value_half, preferred_element_type=jnp....  18.7 us
    dot_general x1, matrix products, per_device(): jnp.dot(row_tokens, qkv_weight, preferred_element_type=jnp.float32)  15.7 us
  transfers between devices with their start and end apart: 5, of which 4 were waited for; matrix products, arithmetic and copies ran while one was open for 22% of the time, Pallas kernels for 0%

commit v1 on v0

--- a/solution.py
+++ b/solution.py
@@ -8,6 +8,27 @@
 HEADS = 16
 GRID = 32
 MASK_SHIFT = 1000000.0
+
+
+def collect(shard, axis, dim):
+    size, position, width = (lax.axis_size(axis), lax.axis_index(axis), shard.shape[dim])
+    right = [(i, (i + 1) % size) for i in range(size)]
+    downward = [(i, (i - 1) % size) for i in range(size)]
+    result = jnp.zeros((*shard.shape[:dim], size * width, *shard.shape[dim + 1 :]), shard.dtype)
+    result = lax.dynamic_update_slice_in_dim(result, shard, position * width, axis=dim)
+    from_left = from_right = shard
+    middle = size // 2
+    for step in range(1, middle + 1):
+        from_left = lax.ppermute(from_left, axis, right)
+        result = lax.dynamic_update_slice_in_dim(
+            result, from_left, (position - step) % size * width, axis=dim
+        )
+        if step < size - middle:
+            from_right = lax.ppermute(from_right, axis, downward)
+            result = lax.dynamic_update_slice_in_dim(
+                result, from_right, (position + step) % size * width, axis=dim
+            )
+    return result
 
 
 def attend_dense(query_norm, key_norm, value_half, row_segments, block_len, scale):
@@ -61,7 +82,7 @@
     normed = (
         tokens * lax.rsqrt(jnp.mean(tokens * tokens, axis=-1, keepdims=True) + 1e-06) * norm_gain
     ).astype(jnp.bfloat16)
-    row_tokens = lax.all_gather(normed, "seq", axis=0, tiled=True)
+    row_tokens = collect(normed, "seq", 0)
     length = row_tokens.shape[0]
     heads_here = qkv_weight.shape[1] // (3 * HEAD_DIM)
     projected = jnp.dot(row_tokens, qkv_weight, preferred_element_type=jnp.float32).reshape(

time: 405 us -> 470 us (1.16)
  waiting for transfers between devices: 201 us -> 231 us
  local copies, waits for them, and re-layouts: 29 us -> 48 us
  starting transfers between devices: 14.9 us -> 28.5 us
    ppermute x0 -> x7, waiting for transfers between devices: none -> 104 us  [the longest x4 104 us: collect(): from_left = lax.ppermute(from_left, axis, right)]
    all_gather x1 -> x0, waiting for transfers between devices: 72.5 us -> none  [per_device(): row_tokens = lax.all_gather(normed, 'seq', axis=0, tiled=True)]
    dynamic_update_slice x0 -> x7, local copies, waits for them, and re-layouts: none -> 13.4 us  [the longest x4 8.1 us: collect(): lax.dynamic_update_slice_in_dim(result, from_left, (position - step) % si...]
    ppermute x0 -> x7, starting transfers between devices: none -> 13 us  [the longest x4 10 us: collect(): from_left = lax.ppermute(from_left, axis, right)]
    broadcast_in_dim x0 -> x1, local copies, waits for them, and re-layouts: none -> 5.6 us  [collect(): jnp.zeros((*shard.shape[:dim], size * width, *shard.shape[dim + 1:]), sha...]
  transfers between devices with their start and end apart: 5 -> 11, of which waited for: 4 -> 7; matrix products, arithmetic and copies ran while one was open for 22% -> 22% of each run, Pallas kernels for 0% -> 0%
where the time goes in v1:
time: 470 us; the launch traced here: 469 us
  waiting for transfers between devices  231 us (49%)
  matrix products  96.4 us (21%)
  local copies, waits for them, and re-layouts  48 us (10%)
  starting transfers between devices  28.5 us (6%)
  other arithmetic  26.7 us (6%)
  blocking collectives  23.9 us (5%)
  between operations  13.6 us (3%)
    ppermute x4, waiting for transfers between devices, collect(): from_left = lax.ppermute(from_left, axis, right)  104 us
    reduce_scatter x1, waiting for transfers between devices, per_device(): lax.psum_scatter(partial.reshape(row_count * merged_count, -1), 'rows', s...  95.1 us
    sub x4, matrix products, one_block(): exp_terms = jnp.exp(scores - peak_val)  31 us
    psum x1, blocking collectives, per_device(): lax.psum(jnp.stack([jnp.sum(query_raw * query_raw, axis=(1, 2)), jnp.sum(...  23.9 us
    all_to_all x1, waiting for transfers between devices, per_device(): lax.all_to_all(merged_norm, 'rows', split_axis=1, concat_axis=0, tiled=True)  20.2 us
    dot_general x1, matrix products, per_device(): jnp.dot(ordered, fc_weight, preferred_element_type=jnp.float32)  19.2 us
    dot_general x4, matrix products, one_block(): jnp.einsum('hqk,khd->qhd', probs, value_half, preferred_element_type=jnp....  18.7 us
    dot_general x1, matrix products, per_device(): jnp.dot(row_tokens, qkv_weight, preferred_element_type=jnp.float32)  15.7 us
  transfers between devices with their start and end apart: 11, of which 7 were waited for; matrix products, arithmetic and copies ran while one was open for 22% of the time, Pallas kernels for 0%

profile of v1, /device:TPU:1, one launch (start us, length us, event | category | flops | bytes accessed | tf_op | source)
XLA Modules:
  0.0 468.6 jit_solution(11617377997142770810)
XLA Ops:
  6.5 1.8 fusion.28
  8.4 5.6 %broadcast_in_dim.29 = bf16[2048,3200]{1,0:T(8,128)(2,1)} broadcast(bf16[]{:T(256)} %constant.58.clone.1), dimensions={} | broadcast | bytes 13107202 | tf_op jit(solution)/shard_map/broadcast_in_dim | solution.py:17
  14.0 1.7 constant_dynamic-update-slice_fusion.8
  15.7 2.6 collective-permute-start
  18.3 27.1 %collective-permute-done = bf16[256,3200]{1,0:T(8,128)(2,1)S(1)} collective-permute-done((bf16[256,3200]{1,0:T(8,128)(2,1)S(1)}, bf16[256,3200]{1,0:T(8,128)(2,1)S(1)}, u32[]{:S(2)}, u32[]{:S(2)}) %collective-permute-start) | collective-permute-done | bytes 1638432 | tf_op jit(solution)/shard_map/ppermute | solution.py:22
  45.4 2.5 collective-permute-start.2
  47.9 2.0 collective-permute-start.3
  49.8 51.2 %collective-permute-done.2 = bf16[256,3200]{1,0:T(8,128)(2,1)} collective-permute-done((bf16[256,3200]{1,0:T(8,128)(2,1)S(1)}, bf16[256,3200]{1,0:T(8,128)(2,1)}, u32[]{:S(2)}, u32[]{:S(2)}) %collective-permute-start.2) | collective-permute-done | bytes 1638432 | tf_op jit(solution)/shard_map/ppermute | solution.py:22
  101.0 2.6 collective-permute-start.4
  103.6 2.7 constant_dynamic-update-slice_fusion.7
  106.4 1.0 collective-permute-start.5
  107.4 2.7 constant_dynamic-update-slice_fusion.6
  110.1 14.1 %collective-permute-done.4 = bf16[256,3200]{1,0:T(8,128)(2,1)S(1)} collective-permute-done((bf16[256,3200]{1,0:T(8,128)(2,1)}, bf16[256,3200]{1,0:T(8,128)(2,1)S(1)}, u32[]{:S(2)}, u32[]{:S(2)}) %collective-permute-start.4) | collective-permute-done | bytes 1638432 | tf_op jit(solution)/shard_map/ppermute | solution.py:22
  124.2 2.4 collective-permute-start.6
  126.6 2.8 constant_dynamic-update-slice_fusion.5
  129.4 1.3 constant_dynamic-update-slice_fusion.4
  130.7 1.3 constant_dynamic-update-slice_fusion.3
  131.9 1.3 constant_dynamic-update-slice_fusion.2
  133.2 11.4 %collective-permute-done.6 = bf16[256,3200]{1,0:T(8,128)(2,1)S(1)} collective-permute-done((bf16[256,3200]{1,0:T(8,128)(2,1)S(1)}, bf16[256,3200]{1,0:T(8,128)(2,1)S(1)}, u32[]{:S(2)}, u32[]{:S(2)}) %collective-permute-start.6) | collective-permute-done | bytes 1638432 | tf_op jit(solution)/shard_map/ppermute | solution.py:22
  144.6 1.3 constant_dynamic-update-slice_fusion.1
  146.0 15.7 %fusion.75 = f32[2048,768]{0,1:T(8,128)S(1)} fusion(bf16[2048,3200]{1,0:T(8,128)(2,1)} %constant_dynamic-update-slice_fusion.1, bf16[3200,768]{1,0:T(8,128)(2,1)} %param.17), kind=kOutput, calls=%fused_computation.105 | convolution fusion | flops 10066329600 | bytes 24313856 | tf_op jit(solution)/shard_map/dot_general | solution.py:88
  161.8 2.5 fusion.73
  164.3 1.9 copy.44
  166.2 2.9 copy.43
  169.4 1.2 copy-done
  170.7 0.3 multiply_reduce_fusion.1
  171.0 23.9 %psum.7 = f32[3,2048]{1,0:T(4,128)S(1)} all-reduce(f32[3,2048]{1,0:T(4,128)S(1)} %pad_maximum_fusion), channel_id=1, replica_groups=mesh['rows'=16,'seq'=8] {'seq'}, use_global_device_ids=true, to_apply=%region_3.4 | all-reduce | flops 6144 | bytes 49152 | tf_op jit(solution)/shard_map/psum | solution.py:100
  195.1 1.3 copy.45
  196.4 3.0 multiply_convert_fusion
  199.3 1.3 fusion.33
  200.7 53.7 %while.10 = (s32[]{:T(128)}, bf16[4,512,2,128]{3,2,1,0:T(2,128)(2,1)S(1)}, f32[4,512]{1,0:T(4,128)S(1)}, f32[1,2048]{1,0:T(1,128)S(1)}, bf16[4,512,2,128]{3,1,0,...) while((s32[]{:T(128)}, ...), condition=%wide.region_7.8_spmd, body=%wide.region_4.7_spmd.sunk | while | flops 1087506432 | bytes 26237560 | solution.py:53
  200.7 0.7 broadcast_compare_fusion.2
  201.3 7.7 %fusion.91 = (f32[2,512]{1,0:T(2,128)S(1)}, f32[2,512,2048]{2,1,0:T(8,128)}) fusion(pred[512,2048]{1,0:T(8,128)(4,1)S(1)} %broadcast_compare_fusion.2, bf16[2048,2,128]{2,0,1:T(8,128)(2,1)} %get-tuple-element.160, bf16[4,512,2,128]{3,1,0,2:T(8,128)(2,1)} %get-tuple-element.159, s32[]{:T(128)} %get-tuple-element.147), kind=kOutput, calls=%fused_computation.102.clone.1 | convolution fusion | flops 545261568 | bytes 10752512 | tf_op jit(solution)/shard_map/while/body/eval_jaxpr/sub | solution.py:47
  209.1 4.7 fusion.92
  214.1 0.7 broadcast_compare_fusion.2
  214.8 7.7 %fusion.91 = (f32[2,512]{1,0:T(2,128)S(1)}, f32[2,512,2048]{2,1,0:T(8,128)}) fusion(pred[512,2048]{1,0:T(8,128)(4,1)S(1)} %broadcast_compare_fusion.2, bf16[2048,2,128]{2,0,1:T(8,128)(2,1)} %get-tuple-element.160, bf16[4,512,2,128]{3,1,0,2:T(8,128)(2,1)} %get-tuple-element.159, s32[]{:T(128)} %get-tuple-element.147), kind=kOutput, calls=%fused_computation.102.clone.1 | convolution fusion | flops 545261568 | bytes 10752512 | tf_op jit(solution)/shard_map/while/body/eval_jaxpr/sub | solution.py:47
  222.5 4.7 fusion.92
  227.5 0.7 broadcast_compare_fusion.2
  228.2 7.7 %fusion.91 = (f32[2,512]{1,0:T(2,128)S(1)}, f32[2,512,2048]{2,1,0:T(8,128)}) fusion(pred[512,2048]{1,0:T(8,128)(4,1)S(1)} %broadcast_compare_fusion.2, bf16[2048,2,128]{2,0,1:T(8,128)(2,1)} %get-tuple-element.160, bf16[4,512,2,128]{3,1,0,2:T(8,128)(2,1)} %get-tuple-element.159, s32[]{:T(128)} %get-tuple-element.147), kind=kOutput, calls=%fused_computation.102.clone.1 | convolution fusion | flops 545261568 | bytes 10752512 | tf_op jit(solution)/shard_map/while/body/eval_jaxpr/sub | solution.py:47
  235.9 4.7 fusion.92
  240.9 0.7 broadcast_compare_fusion.2
  241.6 7.7 %fusion.91 = (f32[2,512]{1,0:T(2,128)S(1)}, f32[2,512,2048]{2,1,0:T(8,128)}) fusion(pred[512,2048]{1,0:T(8,128)(4,1)S(1)} %broadcast_compare_fusion.2, bf16[2048,2,128]{2,0,1:T(8,128)(2,1)} %get-tuple-element.160, bf16[4,512,2,128]{3,1,0,2:T(8,128)(2,1)} %get-tuple-element.159, s32[]{:T(128)} %get-tuple-element.147), kind=kOutput, calls=%fused_computation.102.clone.1 | convolution fusion | flops 545261568 | bytes 10752512 | tf_op jit(solution)/shard_map/while/body/eval_jaxpr/sub | solution.py:47
  249.3 4.7 fusion.92
  254.3 1.5 reshape_reshape.3
  255.8 7.0 %all-to-all-start = ((bf16[8,256,256]{2,1,0:T(8,128)(2,1)}), bf16[8,256,256]{2,1,0:T(8,128)(2,1)S(1)}, u32[]{:S(2)}, u32[]{:S(2)}) async-start(bf16[8,256,256]{2,1,0:T(8,128)(2,1)} %reshape_reshape.3), calls=%async_computation | async-start | bytes 2097152 | tf_op jit(solution)/shard_map/all_to_all | solution.py:123
  262.9 2.8 reshape.214
  265.9 12.1 %all-to-all-done = bf16[8,256,256]{2,1,0:T(8,128)(2,1)S(1)} async-done(((bf16[8,256,256]{2,1,0:T(8,128)(2,1)}), bf16[8,256,256]{2,1,0:T(8,128)(2,1)S(1)}, u32[]{:S(2)}, u32[]{:S(2)}) %all-to-all-start) | async-done | bytes 1048608 | tf_op jit(solution)/shard_map/all_to_all | solution.py:123
  278.0 10.6 %convert_reduce_fusion = f32[256,3200]{1,0:T(8,128)} fusion(bf16[8,256,256]{2,1,0:T(8,128)(2,1)S(1)} %all-to-all-done, bf16[8,256,3200]{2,1,0:T(8,128)(2,1)} %bitcast.100), kind=kOutput, calls=%fused_computation.24 | convolution fusion | flops 3374284800 | bytes 17432576 | tf_op jit(solution)/shard_map/gtc,gcd->gtd/dot_general | solution.py:125
  288.5 5.3 %reduce_sum.69 = f32[4,2,16,2,3200]{4,3,2,1,0:T(2,128)} reshape(f32[256,3200]{1,0:T(8,128)} %convert_reduce_fusion) | data formatting | bytes 6553600 | tf_op jit(solution)/shard_map/reduce_sum | solution.py:128
  293.9 4.2 fusion.66
  298.4 1.9 multiply_reduce_fusion
  300.5 4.5 reshape.212
  305.0 2.7 add_convert_fusion.1
  307.7 1.7 copy.37
  309.4 8.4 %all-to-all-start.1 = ((bf16[64,16,800]{2,0,1:T(8,128)(2,1)}), bf16[64,16,800]{2,0,1:T(8,128)(2,1)S(1)}, u32[]{:S(2)}, u32[]{:S(2)}) async-start(bf16[64,16,800]{2,0,1:T(8,128)(2,1)} %copy.37), calls=%async_computation.1 | async-start | bytes 3670016 | tf_op jit(solution)/shard_map/all_to_all | solution.py:147
  317.9 0.5 broadcast.195
  318.4 0.7 reduce.16
  319.4 0.6 dynamic_slice.11
  319.9 0.6 compare_convert_fusion
  320.7 20.2 %all-to-all-done.1 = bf16[64,16,800]{2,0,1:T(8,128)(2,1)S(1)} async-done(((bf16[64,16,800]{2,0,1:T(8,128)(2,1)}), bf16[64,16,800]{2,0,1:T(8,128)(2,1)S(1)}, u32[]{:S(2)}, u32[]{:S(2)}) %all-to-all-start.1) | async-done | bytes 1638432 | tf_op jit(solution)/shard_map/all_to_all | solution.py:147
  340.8 1.3 fusion.38
  342.1 19.2 %add_convert_fusion = bf16[16,64,6144]{2,1,0:T(8,128)(2,1)} fusion(f32[16,64]{1,0:T(8,128)S(1)} %broadcast_multiply_fusion, bf16[800,6144]{1,0:T(8,128)(2,1)} %param.25, bf16[16,64,800]{2,0,1:T(8,128)(2,1)S(1)} %fusion.38), kind=kOutput, calls=%fused_computation.25 | convolution fusion | flops 10078912512 | bytes 24055808 | tf_op jit(solution)/shard_map/dot_general | solution.py:158
  361.4 95.1 %reduce-scatter.2.cloned.1.call-done = bf16[64,6144]{1,0:T(8,128)(2,1)} async-done(((bf16[1024,6144]{1,0:T(8,128)(2,1)}), bf16[64,6144]{1,0:T(8,128)(2,1)}) %reduce-scatter.2.cloned.1.call-update) | async-done | bytes 786448 | tf_op jit(solution)/shard_map/reduce_scatter | solution.py:164
  456.5 5.2 %fusion.54 = bf16[1,64,6144]{2,1,0:T(8,128)(2,1)} fusion(bf16[64,6144]{1,0:T(8,128)(2,1)} %reduce-scatter.2.cloned.1.call-done, f32[6144]{0:T(1024)S(1)} %copy-done.9), kind=kLoop, calls=%fused_computation.70 | loop fusion | flops 26345472 | bytes 1597440 | tf_op jit(solution)/shard_map/broadcast_in_dim | solution.py:168
  (76 shorter events, 3.1 us)
Async XLA Ops:
  6.5 271.4 %all-gather.3.cloned.1.call-start = ((), (), s32[]{:S(2)}) async-start(), calls=%async_computation.4 | async-start | bytes 14745600 | tf_op jit(solution)/shard_map/all_gather | solution.py:124
  8.4 5.6 %copy-start.1 = (bf16[1,256,3200]{2,1,0:T(8,128)(2,1)S(1)}, bf16[1,256,3200]{2,1,0:T(8,128)(2,1)}, u32[]{:S(2)}) copy-start(bf16[1,256,3200]{2,1,0:T(8,128)(2,1)} %param.15) | copy-start | bytes 4915204
  8.4 5.6 %copy-start.10 = (f32[3200]{0:T(1024)S(1)}, f32[3200]{0:T(1024)}, u32[]{:S(2)}) copy-start(f32[3200]{0:T(1024)} %param.16) | copy-start | bytes 38404
  15.7 87.9 %copy-start.13 = (s32[1,256]{1,0:T(1,128)S(1)}, s32[1,256]{1,0:T(1,128)}, u32[]{:S(2)}) copy-start(s32[1,256]{1,0:T(1,128)} %param.21) | copy-start | bytes 3076
  15.7 88.0 %copy-start.12 = (f32[2,256]{1,0:T(2,128)S(1)}, f32[2,256]{1,0:T(2,128)}, u32[]{:S(2)}) copy-start(f32[2,256]{1,0:T(2,128)} %param.18) | copy-start | bytes 6148
  15.7 29.7 %collective-permute-start = (bf16[256,3200]{1,0:T(8,128)(2,1)S(1)}, bf16[256,3200]{1,0:T(8,128)(2,1)S(1)}, u32[]{:S(2)}, u32[]{:S(2)}) collective-permute-start(bf16[256,3200]{1,0:T(8,128)(2,1)S(1)} %get-tuple-element.83), channel_id=1, source_target_pairs={{0,1},{1,2},{2,3},{3,4},{4,5},{5,6},{6,7},{7,0},{8,9},{9,10},{10,1... | collective-permute-start | bytes 4915208 | tf_op jit(solution)/shard_map/ppermute | solution.py:22
  18.3 29.6 %collective-permute-start.1 = (bf16[256,3200]{1,0:T(8,128)(2,1)S(1)}, bf16[256,3200]{1,0:T(8,128)(2,1)}, u32[]{:S(2)}, u32[]{:S(2)}) collective-permute-start(bf16[256,3200]{1,0:T(8,128)(2,1)S(1)} %get-tuple-element.83), channel_id=1, source_target_pairs={{0,7},{1,0},{2,1},{3,2},{4,3},{5,4},{6,5},{7,6},{8,15},{9,8},{10,9... | collective-permute-start | bytes 4915208 | tf_op jit(solution)/shard_map/ppermute | solution.py:27
  45.4 4.4 copy-start.4
  45.4 55.6 %collective-permute-start.2 = (bf16[256,3200]{1,0:T(8,128)(2,1)S(1)}, bf16[256,3200]{1,0:T(8,128)(2,1)}, u32[]{:S(2)}, u32[]{:S(2)}) collective-permute-start(bf16[256,3200]{1,0:T(8,128)(2,1)S(1)} %collective-permute-done), channel_id=1, source_target_pairs={{0,1},{1,2},{2,3},{3,4},{4,5},{5,6},{6,7},{7,0},{8,9},{9,10},{10,1... | collective-permute-start | bytes 4915208 | tf_op jit(solution)/shard_map/ppermute | solution.py:22
  47.9 58.5 %collective-permute-start.3 = (bf16[256,3200]{1,0:T(8,128)(2,1)}, bf16[256,3200]{1,0:T(8,128)(2,1)S(1)}, u32[]{:S(2)}, u32[]{:S(2)}) collective-permute-start(bf16[256,3200]{1,0:T(8,128)(2,1)} %collective-permute-done.1), channel_id=1, source_target_pairs={{0,7},{1,0},{2,1},{3,2},{4,3},{5,4},{6,5},{7,6},{8,15},{9,8},{10,9... | collective-permute-start | bytes 4915208 | tf_op jit(solution)/shard_map/ppermute | solution.py:27
  101.0 23.2 %collective-permute-start.4 = (bf16[256,3200]{1,0:T(8,128)(2,1)}, bf16[256,3200]{1,0:T(8,128)(2,1)S(1)}, u32[]{:S(2)}, u32[]{:S(2)}) collective-permute-start(bf16[256,3200]{1,0:T(8,128)(2,1)} %collective-permute-done.2), channel_id=1, source_target_pairs={{0,1},{1,2},{2,3},{3,4},{4,5},{5,6},{6,7},{7,0},{8,9},{9,10},{10,1... | collective-permute-start | bytes 4915208 | tf_op jit(solution)/shard_map/ppermute | solution.py:22
  106.4 25.6 %collective-permute-start.5 = (bf16[256,3200]{1,0:T(8,128)(2,1)S(1)}, bf16[256,3200]{1,0:T(8,128)(2,1)S(1)}, u32[]{:S(2)}, u32[]{:S(2)}) collective-permute-start(bf16[256,3200]{1,0:T(8,128)(2,1)S(1)} %collective-permute-done.3), channel_id=1, source_target_pairs={{0,7},{1,0},{2,1},{3,2},{4,3},{5,4},{6,5},{7,6},{8,15},{9,8},{10,9... | collective-permute-start | bytes 4915208 | tf_op jit(solution)/shard_map/ppermute | solution.py:27
  124.2 20.4 %collective-permute-start.6 = (bf16[256,3200]{1,0:T(8,128)(2,1)S(1)}, bf16[256,3200]{1,0:T(8,128)(2,1)S(1)}, u32[]{:S(2)}, u32[]{:S(2)}) collective-permute-start(bf16[256,3200]{1,0:T(8,128)(2,1)S(1)} %collective-permute-done.4), channel_id=1, source_target_pairs={{0,1},{1,2},{2,3},{3,4},{4,5},{5,6},{6,7},{7,0},{8,9},{9,10},{10,1... | collective-permute-start | bytes 4915208 | tf_op jit(solution)/shard_map/ppermute | solution.py:22
  169.1 1.6 copy-start
  199.3 1.3 copy-start.5
  201.3 7.8 %copy-start.6 = (bf16[2048,2,128]{2,0,1:T(8,128)(2,1)S(1)}, bf16[2048,2,128]{2,0,1:T(8,128)(2,1)}, u32[]{:S(2)}) copy-start(bf16[2048,2,128]{2,0,1:T(8,128)(2,1)} %get-tuple-element.161) | copy-start | bytes 3145732 | tf_op jit(solution)/shard_map/while
  214.7 7.8 %copy-start.6 = (bf16[2048,2,128]{2,0,1:T(8,128)(2,1)S(1)}, bf16[2048,2,128]{2,0,1:T(8,128)(2,1)}, u32[]{:S(2)}) copy-start(bf16[2048,2,128]{2,0,1:T(8,128)(2,1)} %get-tuple-element.161) | copy-start | bytes 3145732 | tf_op jit(solution)/shard_map/while
  228.2 7.8 %copy-start.6 = (bf16[2048,2,128]{2,0,1:T(8,128)(2,1)S(1)}, bf16[2048,2,128]{2,0,1:T(8,128)(2,1)}, u32[]{:S(2)}) copy-start(bf16[2048,2,128]{2,0,1:T(8,128)(2,1)} %get-tuple-element.161) | copy-start | bytes 3145732 | tf_op jit(solution)/shard_map/while
  241.6 7.8 %copy-start.6 = (bf16[2048,2,128]{2,0,1:T(8,128)(2,1)S(1)}, bf16[2048,2,128]{2,0,1:T(8,128)(2,1)}, u32[]{:S(2)}) copy-start(bf16[2048,2,128]{2,0,1:T(8,128)(2,1)} %get-tuple-element.161) | copy-start | bytes 3145732 | tf_op jit(solution)/shard_map/while
  254.3 8.5 %copy-start.2 = (bf16[1,256,3200]{2,1,0:T(8,128)(2,1)S(1)}, bf16[1,256,3200]{2,1,0:T(8,128)(2,1)}, u32[]{:S(2)}) copy-start(bf16[1,256,3200]{2,1,0:T(8,128)(2,1)} %param.15) | copy-start | bytes 4915204
  255.8 22.1 %all-to-all-start = ((bf16[8,256,256]{2,1,0:T(8,128)(2,1)}), bf16[8,256,256]{2,1,0:T(8,128)(2,1)S(1)}, u32[]{:S(2)}, u32[]{:S(2)}) async-start(bf16[8,256,256]{2,1,0:T(8,128)(2,1)} %reshape_reshape.3), calls=%async_computation | async-start | bytes 2097152 | tf_op jit(solution)/shard_map/all_to_all | solution.py:123
  262.8 2.8 copy-start.7
  262.8 2.9 copy-start.8
  288.5 5.3 %copy-start.3 = (f32[4,2,16,2,3200]{4,3,2,1,0:T(2,128)S(1)}, f32[4,2,16,2,3200]{4,3,2,1,0:T(2,128)}, u32[]{:S(2)}) copy-start(f32[4,2,16,2,3200]{4,3,2,1,0:T(2,128)} %reshape.214) | copy-start | bytes 9830404
  288.5 5.3 %copy-start.11 = (f32[3200]{0:T(1024)S(1)}, f32[3200]{0:T(1024)}, u32[]{:S(2)}) copy-start(f32[3200]{0:T(1024)} %param.20) | copy-start | bytes 38404
  309.4 9.0 %copy-start.14 = (s32[1,256]{1,0:T(1,128)S(1)}, s32[1,256]{1,0:T(1,128)}, u32[]{:S(2)}) copy-start(s32[1,256]{1,0:T(1,128)} %param.22) | copy-start | bytes 3076
  309.4 10.0 %copy-start.15 = (s32[16]{0:T(128)S(1)}, s32[16]{0:T(128)}, u32[]{:S(2)}) copy-start(s32[16]{0:T(128)} %param.27) | copy-start | bytes 196
  309.4 31.5 %all-to-all-start.1 = ((bf16[64,16,800]{2,0,1:T(8,128)(2,1)}), bf16[64,16,800]{2,0,1:T(8,128)(2,1)S(1)}, u32[]{:S(2)}, u32[]{:S(2)}) async-start(bf16[64,16,800]{2,0,1:T(8,128)(2,1)} %copy.37), calls=%async_computation.1 | async-start | bytes 3670016 | tf_op jit(solution)/shard_map/all_to_all | solution.py:147
  317.8 138.7 %reduce-scatter.2.cloned.1.call-start = ((), (), s32[]{:S(2)}) async-start(), calls=%async_computation.3 | async-start | bytes 13369344 | tf_op jit(solution)/shard_map/reduce_scatter | solution.py:164
  361.4 95.2 %copy-start.9 = (f32[6144]{0:T(1024)S(1)}, f32[6144]{0:T(1024)}, u32[]{:S(2)}) copy-start(f32[6144]{0:T(1024)} %param.26) | copy-start | bytes 73732
Sparse Core Ops, SparseCore 0:
  18.4 93.5 all-gather.2
  361.5 94.9 reduce-scatter.1
